TPU v7x, 256 devices: a whole 4x4x8 slice. The times are simulated.
256 devices in a mesh: view: 4 (over y_hi, core), row: 8 (over z), col: 8 (over y_lo, x).
Axes of the slice: x: 4, y: 4 (y_hi: 2, y_lo: 2; y = y_hi * 2 + y_lo), z: 8, core: 2. Of those that a mesh axis runs over, the one named last changes fastest.
Arguments:
- view_maps: bfloat16 [16, 32, 128, 768], P('view', 'row', 'col'), may hold values from -6 to 6
- gain_spatial: float32 [768], replicated, may hold values from 0.1 to 1.9
- spatial_query: bfloat16 [768, 768], replicated, may hold values from -8 to 8
- spatial_key: bfloat16 [768, 768], replicated, may hold values from -8 to 8
- spatial_value: bfloat16 [768, 768], replicated, may hold values from -0.21875 to 0.21875
- spatial_output: bfloat16 [768, 768], replicated, may hold values from -0.21875 to 0.21875
- gain_temporal: float32 [768], replicated, may hold values from 0.1 to 1.9
- temporal_query: bfloat16 [768, 768], replicated, may hold values from -8 to 8
- temporal_key: bfloat16 [768, 768], replicated, may hold values from -8 to 8
- temporal_value: bfloat16 [768, 768], replicated, may hold values from -0.21875 to 0.21875
- temporal_output: bfloat16 [768, 768], replicated, may hold values from -0.21875 to 0.21875
Outputs:
- refined: bfloat16 [16, 32, 128, 768], P('view', 'row', 'col')
All inputs are finite; a program needn't handle non-finite values.
Results may differ from a plain program's by a relative error of at most 0.012.
Values may be sent and summed in bfloat16 or wider, within the bound.
No kernel may reach another device: no remote copies, remote signals or barrier semaphores. Data moves between devices by JAX's collectives and lax.ppermute only.
A program may use at most 64 MiB of HBM per device.

v0:
```python
import jax
import jax.numpy as jnp
from jax import lax
from jax.sharding import PartitionSpec as P

HEADS = 12
HEAD_DIM = 64
RADIUS = 3
epsilon = 1e-06
very_negative = -1e30


def padded(block, sides, width):
    for axis, dim in sides:
        count = lax.axis_size(axis)
        forward = [(i, i + 1) for i in range(count - 1)]
        backward = [(target, source) for source, target in forward]
        low = lax.ppermute(
            lax.slice_in_dim(block, block.shape[dim] - width, None, axis=dim), axis, forward
        )
        high = lax.ppermute(lax.slice_in_dim(block, 0, width, axis=dim), axis, backward)
        block = jnp.concatenate([low, block, high], axis=dim)
    return block


def rms_norm(tokens, gain_vector):
    values = tokens.astype(jnp.float32)
    scaled = values * lax.rsqrt(jnp.mean(values * values, axis=-1, keepdims=True) + epsilon)
    return (scaled * gain_vector).astype(jnp.bfloat16)


def project(tokens, weight_matrix):
    flat = tokens.reshape(-1, tokens.shape[-1])
    result = jnp.dot(flat, weight_matrix, preferred_element_type=jnp.float32)
    return result.reshape(tokens.shape[:-1] + (weight_matrix.shape[1],))


def grid_rows(count_rows, count_cols):
    return jnp.broadcast_to(
        jnp.arange(count_rows, dtype=jnp.int32)[:, None], (count_rows, count_cols)
    ).reshape(-1)


def grid_cols(count_rows, count_cols):
    return jnp.broadcast_to(
        jnp.arange(count_cols, dtype=jnp.int32)[None, :], (count_rows, count_cols)
    ).reshape(-1)


def neighbour(queries, keys_wide, values_wide, first_row, first_col, total_rows, total_cols):
    local_views, height, width, features = queries.shape
    wide_rows, wide_cols = (keys_wide.shape[1], keys_wide.shape[2])
    factor = HEAD_DIM ** (-0.5)
    query_rows = grid_rows(height, width)
    query_cols = grid_cols(height, width)
    key_rows = grid_rows(wide_rows, wide_cols)
    key_cols = grid_cols(wide_rows, wide_cols)
    row_gap = key_rows[None, :] - RADIUS - query_rows[:, None]
    col_gap = key_cols[None, :] - RADIUS - query_cols[:, None]
    in_band = (jnp.abs(row_gap) <= RADIUS) & (jnp.abs(col_gap) <= RADIUS)
    global_rows = first_row - RADIUS + key_rows
    global_cols = first_col - RADIUS + key_cols
    inside = (
        (global_rows >= 0)
        & (global_rows < total_rows)
        & (global_cols >= 0)
        & (global_cols < total_cols)
    )
    allowed = (in_band & inside[None, :])[None, :, :]

    def one_view(items):
        query_heads = items[0].reshape(height * width, HEADS, HEAD_DIM)
        key_heads = items[1].reshape(wide_rows * wide_cols, HEADS, HEAD_DIM)
        value_heads = items[2].reshape(wide_rows * wide_cols, HEADS, HEAD_DIM).astype(jnp.float32)
        scores = (
            jnp.einsum("qhe,khe->hqk", query_heads, key_heads, preferred_element_type=jnp.float32)
            * factor
        )
        scores = jnp.where(allowed, scores, very_negative)
        highest = jnp.max(scores, axis=-1, keepdims=True)
        weights = jnp.exp(scores - highest)
        weights = weights / jnp.sum(weights, axis=-1, keepdims=True)
        mixed = jnp.einsum("hqk,khe->qhe", weights, value_heads, precision=lax.Precision.HIGHEST)
        return mixed.reshape(height, width, features).astype(jnp.bfloat16)

    return lax.map(one_view, (queries, keys_wide, values_wide))


def body(
    view_maps,
    gain_spatial,
    spatial_query,
    spatial_key,
    spatial_value,
    spatial_output,
    gain_temporal,
    temporal_query,
    temporal_key,
    temporal_value,
    temporal_output,
):
    local_views, tile_rows, tile_cols = (view_maps.shape[0], view_maps.shape[1], view_maps.shape[2])
    total_rows = lax.axis_size("row") * tile_rows
    total_cols = lax.axis_size("col") * tile_cols
    first_row = lax.axis_index("row") * tile_rows
    first_col = lax.axis_index("col") * tile_cols
    normed = rms_norm(view_maps, gain_spatial)
    queries = project(normed, spatial_query).astype(jnp.bfloat16)
    keys = project(normed, spatial_key).astype(jnp.bfloat16)
    values = project(normed, spatial_value).astype(jnp.bfloat16)
    stacked = jnp.stack([keys, values], 0)
    widened = padded(stacked, (("row", 2), ("col", 3)), RADIUS)
    keys_wide = widened[0]
    values_wide = widened[1]
    attended = neighbour(
        queries, keys_wide, values_wide, first_row, first_col, total_rows, total_cols
    )
    middle = (view_maps.astype(jnp.float32) + project(attended, spatial_output)).astype(
        jnp.bfloat16
    )
    normed_time = rms_norm(middle, gain_temporal)
    factor = HEAD_DIM ** (-0.5)
    positions = tile_rows * tile_cols
    query_time = project(normed_time, temporal_query).astype(jnp.bfloat16)
    key_time = project(normed_time, temporal_key).astype(jnp.bfloat16)
    value_time = project(normed_time, temporal_value).astype(jnp.bfloat16)
    query_heads = query_time.reshape(local_views, positions, HEADS, HEAD_DIM)
    running_max = jnp.full((local_views, positions, HEADS), very_negative, jnp.float32)
    key_heads = lax.all_gather(key_time, "view", axis=0, tiled=True).reshape(
        -1, positions, HEADS, HEAD_DIM
    )
    value_heads = (
        lax.all_gather(value_time, "view", axis=0, tiled=True)
        .reshape(-1, positions, HEADS, HEAD_DIM)
        .astype(jnp.float32)
    )
    scores = (
        jnp.einsum("qphe,kphe->qkph", query_heads, key_heads, preferred_element_type=jnp.float32)
        * factor
    )
    new_max = jnp.maximum(running_max, jnp.max(scores, axis=1))
    weights = jnp.exp(scores - new_max[:, None])
    new_sum = jnp.sum(weights, axis=1)
    new_acc = jnp.einsum("qkph,kphe->qphe", weights, value_heads)
    attended_time = (new_acc / new_sum[..., None]).reshape(view_maps.shape).astype(jnp.bfloat16)
    refined = (middle.astype(jnp.float32) + project(attended_time, temporal_output)).astype(
        jnp.bfloat16
    )
    return refined


def solution(mesh):
    return jax.shard_map(
        body,
        mesh=mesh,
        in_specs=(P("view", "row", "col", None), P(), P(), P(), P(), P(), P(), P(), P(), P(), P()),
        out_specs=P("view", "row", "col", None),
        check_vma=False,
    )
```

profile of v0, /device:TPU:1, one launch (start us, length us, event | category | flops | bytes accessed | tf_op | source)
XLA Modules:
  0.0 165.9 jit_solution(17304333860771478719)
XLA Ops:
  6.6 1.3 fusion.40
  7.9 1.9 %fusion.28 = bf16[1,4,4,16,768]{4,3,2,1,0:T(8,128)(2,1)S(1)} fusion(bf16[768,768]{1,0:T(8,128)(2,1)} %param.16, bf16[4,4,16,768]{3,2,1,0:T(8,128)(2,1)} %param.13, f32[768]{0:T(1024)} %param.14, f32[4,4,16]{2,1,0:T(4,128)S(1)} %add_rsqrt_fusion.1), kind=kOutput, calls=%fused_computation.46 | convolution fusion | flops 302972928 | bytes 1970176 | tf_op jit(solution)/shard_map/dot_general | solution.py:34
  9.9 0.5 fusion.29
  10.4 1.1 fusion.45
  11.5 4.4 %collective-permute-start = (bf16[2,4,3,16,768]{4,3,2,1,0:T(8,128)(2,1)}, bf16[2,4,3,16,768]{4,3,2,1,0:T(8,128)(2,1)S(1)}, u32[]{:S(2)}, u32[]{:S(2)}) collective-permute-start(bf16[2,4,3,16,768]{4,3,2,1,0:T(8,128)(2,1)} %get-tuple-element.103), channel_id=1, source_target_pairs={{0,8},{8,16},{16,24},{24,32},{32,40},{40,48},{48,56},{1,9},{9,17},... | collective-permute-start | bytes 1769480 | tf_op jit(solution)/shard_map/ppermute | solution.py:18
  15.9 1.3 collective-permute-start.1
  17.2 0.6 reshape.291
  18.0 10.2 %collective-permute-done = bf16[2,4,3,16,768]{4,3,2,1,0:T(8,128)(2,1)S(1)} collective-permute-done((bf16[2,4,3,16,768]{4,3,2,1,0:T(8,128)(2,1)}, bf16[2,4,3,16,768]{4,3,2,1,0:T(8,128)(2,1)S(1)}, u32[]{:S(2)}, u32[]{:S(2)}) %collective-permute-start) | collective-permute-done | bytes 589856 | tf_op jit(solution)/shard_map/ppermute | solution.py:18
  28.2 4.1 %collective-permute-done.1 = bf16[2,4,3,16,768]{4,3,2,1,0:T(8,128)(2,1)S(1)} collective-permute-done((bf16[2,4,3,16,768]{4,3,2,1,0:T(8,128)(2,1)}, bf16[2,4,3,16,768]{4,3,2,1,0:T(8,128)(2,1)S(1)}, u32[]{:S(2)}, u32[]{:S(2)}) %collective-permute-start.1) | collective-permute-done | bytes 589856 | tf_op jit(solution)/shard_map/ppermute | solution.py:21
  32.2 1.3 pad_maximum_fusion.5
  33.6 3.9 %collective-permute-start.2 = (bf16[2,4,10,3,768]{4,3,2,1,0:T(4,128)(2,1)}, bf16[2,4,10,3,768]{4,3,2,1,0:T(4,128)(2,1)}, u32[]{:S(2)}, u32[]{:S(2)}) collective-permute-start(bf16[2,4,10,3,768]{4,3,2,1,0:T(4,128)(2,1)} %get-tuple-element.101), channel_id=1, source_target_pairs={{0,1},{1,2},{2,3},{3,4},{4,5},{5,6},{6,7},{8,9},{9,10},{10,11},{11... | collective-permute-start | bytes 1105928 | tf_op jit(solution)/shard_map/ppermute | solution.py:18
  37.5 1.3 collective-permute-start.3
  38.9 0.6 broadcast_in_dim.38
  39.5 0.7 sub.85
  40.3 2.6 %convolution_convert_fusion.4 = bf16[4,4,16,768]{3,2,1,0:T(8,128)(2,1)} fusion(bf16[768,768]{1,0:T(8,128)(2,1)} %param.15, bf16[4,4,16,768]{3,2,1,0:T(8,128)(2,1)S(1)} %copy-done.2, f32[768]{0:T(1024)} %param.14, f32[4,4,16]{2,1,0:T(4,128)} %copy-done.4), kind=kOutput, calls=%fused_computation.43 | convolution fusion | flops 302972928 | bytes 1970176 | tf_op jit(solution)/shard_map/dot_general | solution.py:34
  42.8 3.1 %collective-permute-done.2 = bf16[2,4,10,3,768]{4,3,2,1,0:T(4,128)(2,1)} collective-permute-done((bf16[2,4,10,3,768]{4,3,2,1,0:T(4,128)(2,1)}, bf16[2,4,10,3,768]{4,3,2,1,0:T(4,128)(2,1)}, u32[]{:S(2)}, u32[]{:S(2)}) %collective-permute-start.2) | collective-permute-done | bytes 368672 | tf_op jit(solution)/shard_map/ppermute | solution.py:18
  45.9 4.6 %collective-permute-done.3 = bf16[2,4,10,3,768]{4,3,2,1,0:T(4,128)(2,1)} collective-permute-done((bf16[2,4,10,3,768]{4,3,2,1,0:T(4,128)(2,1)}, bf16[2,4,10,3,768]{4,3,2,1,0:T(4,128)(2,1)}, u32[]{:S(2)}, u32[]{:S(2)}) %collective-permute-start.3) | collective-permute-done | bytes 368672 | tf_op jit(solution)/shard_map/ppermute | solution.py:21
  50.5 3.1 %pad_maximum_fusion = bf16[2,4,10,22,768]{4,3,2,1,0:T(8,128)(2,1)S(1)} fusion(bf16[2,4,10,3,768]{4,3,2,1,0:T(4,128)(2,1)} %collective-permute-done.3, bf16[2,4,3,16,768]{4,3,2,1,0:T(8,128)(2,1)S(1)} %collective-permute-done.1, bf16[1,4,4,16,768]{4,3,2,1,0:T(8,128)(2,1)S(1)} %fusion.29, bf16[1,4,4,16,768]{4,3,2,1,0:T(8,128)(2,1)S(1)} %fusion.28, ...), kind=kLoop, calls=%fused_computation.26 | loop fusion | flops 16220160 | bytes 5406720 | tf_op jit(solution)/shard_map/concatenate | solution.py:22
  53.6 1.8 %slice_bitcast_fusion = (bf16[4,10,22,768]{3,2,1,0:T(8,128)(2,1)}, bf16[4,10,22,768]{3,2,1,0:T(8,128)(2,1)}) fusion(bf16[2,4,10,22,768]{4,3,2,1,0:T(8,128)(2,1)S(1)} %pad_maximum_fusion), kind=kLoop, calls=%fused_computation.33 | loop fusion | bytes 5406720 | tf_op jit(solution)/shard_map/squeeze | solution.py:113
  55.4 26.6 %while.11 = (s32[]{:T(128)}, bf16[4,4,16,768]{3,2,1,0:T(8,128)(2,1)}, bf16[4,10,22,768]{3,2,1,0:T(8,128)(2,1)}, bf16[4,4,16,768]{3,2,1,0:T(8,128)(2,1)}, bf16[4,...) while((s32[]{:T(128)}, ...), condition=%wide.region_4.5_spmd.clone, body=%wide.region_1.4_spmd.clone.sunk | while | flops 152731136 | bytes 6633009 | solution.py:86
  55.4 1.1 constant_dynamic-slice_fusion.5
  56.6 0.5 reshape.306
  57.2 0.9 constant_dynamic-slice_fusion.6
  58.3 0.6 fusion.71
  59.0 0.3 fusion.72
  59.3 0.5 reshape.308
  59.9 1.2 fusion.73
  61.4 0.7 constant_dynamic-update-slice_fusion.2
  62.1 1.1 constant_dynamic-slice_fusion.5
  63.2 0.5 reshape.306
  63.9 0.9 constant_dynamic-slice_fusion.6
  65.0 0.6 fusion.71
  66.0 0.5 reshape.308
  66.5 1.2 fusion.73
  68.1 0.7 constant_dynamic-update-slice_fusion.2
  68.8 1.1 constant_dynamic-slice_fusion.5
  69.9 0.5 reshape.306
  70.6 0.9 constant_dynamic-slice_fusion.6
  71.6 0.6 fusion.71
  72.6 0.5 reshape.308
  73.2 1.2 fusion.73
  74.8 0.7 constant_dynamic-update-slice_fusion.2
  75.4 1.1 constant_dynamic-slice_fusion.5
  76.6 0.5 reshape.306
  77.2 0.9 constant_dynamic-slice_fusion.6
  78.3 0.6 fusion.71
  79.3 0.5 reshape.308
  79.8 1.2 fusion.73
  81.4 0.7 constant_dynamic-update-slice_fusion.2
  82.1 1.8 %multiply_reduce_fusion = (f32[4,4,16]{2,1,0:T(4,128)S(1)}, f32[4,4,16,768]{3,2,1,0:T(8,128)S(1)}) fusion(bf16[4,4,16,768]{3,2,1,0:T(8,128)(2,1)} %get-tuple-element.37, bf16[768,768]{1,0:T(8,128)(2,1)S(1)} %copy-done, bf16[4,4,16,768]{3,2,1,0:T(8,128)(2,1)} %param.13), kind=kOutput, calls=%fused_computation.67 | convolution fusion | flops 303169280 | bytes 2753536 | tf_op jit(solution)/shard_map/dot_general | solution.py:34
  84.0 1.2 convolution_convert_fusion.2
  85.5 1.2 convolution_convert_fusion.3
  86.8 1.7 %convolution_convert_fusion.1 = bf16[4,4,16,768]{3,2,1,0:T(8,128)(2,1)S(1)} fusion(bf16[4,4,16,768]{3,2,1,0:T(8,128)(2,1)S(1)} %multiply_convert_fusion, bf16[768,768]{1,0:T(8,128)(2,1)} %param.20), kind=kOutput, calls=%fused_computation.40 | convolution fusion | flops 302186496 | bytes 1966080 | tf_op jit(solution)/shard_map/dot_general | solution.py:34
  88.6 0.6 reshape.290
  89.2 28.3 %all-gather.5.cloned.1.call-done = bf16[16,4,16,768]{3,2,1,0:T(8,128)(2,1)} async-done(((bf16[4,4,16,768]{3,2,1,0:T(8,128)(2,1)}), bf16[16,4,16,768]{3,2,1,0:T(8,128)(2,1)}) %all-gather.5.cloned.1.call-update) | async-done | bytes 1572880 | tf_op jit(solution)/shard_map/all_gather | solution.py:129
  117.5 5.9 %reshape.289 = bf16[16,64,12,64]{3,2,1,0:T(8,128)(2,1)} reshape(bf16[16,4,16,768]{3,2,1,0:T(8,128)(2,1)} %all-gather.5.cloned.1.call-done) | data formatting | bytes 3145728 | tf_op jit(solution)/shard_map/reshape | solution.py:129
  123.4 5.0 %bitcast_reduce_fusion = (f32[4,64,12]{0,2,1:T(8,128)S(1)}, f32[64,12,16,4]{2,3,1,0:T(4,128)S(1)}) fusion(bf16[4,64,12,64]{3,2,1,0:T(8,128)(2,1)S(1)} %reshape.290, bf16[16,64,12,64]{3,2,1,0:T(8,128)(2,1)} %reshape.289), kind=kOutput, calls=%fused_computation.29 | convolution fusion | flops 6386688 | bytes 2174976 | tf_op jit(solution)/shard_map/qphe,kphe->qkph/dot_general | solution.py:138
  128.4 1.1 copy-done.1
  129.5 1.9 %fusion.30 = f32[4,64,12]{0,2,1:T(8,128)S(1)} fusion(f32[64,12,16,4]{2,3,1,0:T(4,128)S(1)} %get-tuple-element.108, f32[4,64,12]{0,2,1:T(8,128)S(1)} %broadcast_maximum_fusion), kind=kLoop, calls=%fused_computation.48 | loop fusion | flops 95232 | bytes 221184 | tf_op jit(solution)/shard_map/reduce_sum | solution.py:143
  131.4 13.6 %all-gather.3.cloned.1.call-done = bf16[16,4,16,768]{3,2,1,0:T(8,128)(2,1)} async-done(((bf16[4,4,16,768]{3,2,1,0:T(8,128)(2,1)}), bf16[16,4,16,768]{3,2,1,0:T(8,128)(2,1)}) %all-gather.3.cloned.1.call-update) | async-done | bytes 1572880 | tf_op jit(solution)/shard_map/all_gather | solution.py:133
  145.0 5.9 %reshape.288 = bf16[16,64,12,64]{3,2,1,0:T(8,128)(2,1)} reshape(bf16[16,4,16,768]{3,2,1,0:T(8,128)(2,1)} %all-gather.3.cloned.1.call-done) | data formatting | bytes 3145728 | tf_op jit(solution)/shard_map/reshape | solution.py:134
  150.9 4.9 %fusion.19 = bf16[4,64,12,64]{3,0,2,1:T(4,128)(2,1)S(1)} fusion(bf16[16,64,12,64]{3,2,1,0:T(8,128)(2,1)} %reshape.288, f32[64,12,16,4]{2,3,1,0:T(4,128)} %copy-done.1, f32[4,64,12]{0,2,1:T(8,128)S(1)} %fusion.30, f32[4,64,12]{0,2,1:T(8,128)S(1)} %broadcast_maximum_fusion), kind=kOutput, calls=%fused_computation.31 | convolution fusion | flops 6733824 | bytes 2187264 | tf_op jit(solution)/shard_map/qkph,kphe->qphe/dot_general | solution.py:144
  156.0 0.6 convert_element_type.76
  156.6 2.5 %fusion.27 = bf16[4,4,16,768]{3,2,1,0:T(8,128)(2,1)} fusion(f32[4,4,16,768]{3,2,1,0:T(8,128)S(1)} %get-tuple-element.106, bf16[4,4,16,768]{3,2,1,0:T(8,128)(2,1)S(1)} %convert_element_type.76, bf16[768,768]{1,0:T(8,128)(2,1)} %param.23), kind=kOutput, calls=%fused_computation.39 | convolution fusion | flops 302383104 | bytes 2752512 | tf_op jit(solution)/shard_map/dot_general | solution.py:34
  (55 shorter events, 4.7 us)
Async XLA Ops:
  6.5 75.5 %copy-start = (bf16[768,768]{1,0:T(8,128)(2,1)S(1)}, bf16[768,768]{1,0:T(8,128)(2,1)}, u32[]{:S(2)}) copy-start(bf16[768,768]{1,0:T(8,128)(2,1)} %param.18) | copy-start | bytes 3538948
  6.5 3.3 %copy-start.2 = (bf16[4,4,16,768]{3,2,1,0:T(8,128)(2,1)S(1)}, bf16[4,4,16,768]{3,2,1,0:T(8,128)(2,1)}, u32[]{:S(2)}) copy-start(bf16[4,4,16,768]{3,2,1,0:T(8,128)(2,1)} %param.13) | copy-start | bytes 1179652
  6.5 3.3 %copy-start.9 = (f32[768]{0:T(1024)S(1)}, f32[768]{0:T(1024)}, u32[]{:S(2)}) copy-start(f32[768]{0:T(1024)} %param.14) | copy-start | bytes 9220
  6.5 111.0 %all-gather.5.cloned.1.call-start = ((), (), s32[]{:S(2)}) async-start(), calls=%async_computation.1 | async-start | bytes 1966080 | tf_op jit(solution)/shard_map/all_gather | solution.py:129
  6.5 3.3 %copy-start.6 = (bf16[768,768]{1,0:T(8,128)(2,1)S(1)}, bf16[768,768]{1,0:T(8,128)(2,1)}, u32[]{:S(2)}) copy-start(bf16[768,768]{1,0:T(8,128)(2,1)} %param.17) | copy-start | bytes 3538948
  7.9 2.5 %copy-start.4 = (f32[4,4,16]{2,1,0:T(4,128)}, f32[4,4,16]{2,1,0:T(4,128)S(1)}, u32[]{:S(2)}) copy-start(f32[4,4,16]{2,1,0:T(4,128)S(1)} %add_rsqrt_fusion.1) | copy-start | bytes 3076
  11.5 16.7 %collective-permute-start = (bf16[2,4,3,16,768]{4,3,2,1,0:T(8,128)(2,1)}, bf16[2,4,3,16,768]{4,3,2,1,0:T(8,128)(2,1)S(1)}, u32[]{:S(2)}, u32[]{:S(2)}) collective-permute-start(bf16[2,4,3,16,768]{4,3,2,1,0:T(8,128)(2,1)} %get-tuple-element.103), channel_id=1, source_target_pairs={{0,8},{8,16},{16,24},{24,32},{32,40},{40,48},{48,56},{1,9},{9,17},... | collective-permute-start | bytes 1769480 | tf_op jit(solution)/shard_map/ppermute | solution.py:18
  15.9 16.3 %collective-permute-start.1 = (bf16[2,4,3,16,768]{4,3,2,1,0:T(8,128)(2,1)}, bf16[2,4,3,16,768]{4,3,2,1,0:T(8,128)(2,1)S(1)}, u32[]{:S(2)}, u32[]{:S(2)}) collective-permute-start(bf16[2,4,3,16,768]{4,3,2,1,0:T(8,128)(2,1)} %get-tuple-element.104), channel_id=1, source_target_pairs={{8,0},{16,8},{24,16},{32,24},{40,32},{48,40},{56,48},{9,1},{17,9},... | collective-permute-start | bytes 1769480 | tf_op jit(solution)/shard_map/ppermute | solution.py:21
  33.6 12.3 %collective-permute-start.2 = (bf16[2,4,10,3,768]{4,3,2,1,0:T(4,128)(2,1)}, bf16[2,4,10,3,768]{4,3,2,1,0:T(4,128)(2,1)}, u32[]{:S(2)}, u32[]{:S(2)}) collective-permute-start(bf16[2,4,10,3,768]{4,3,2,1,0:T(4,128)(2,1)} %get-tuple-element.101), channel_id=1, source_target_pairs={{0,1},{1,2},{2,3},{3,4},{4,5},{5,6},{6,7},{8,9},{9,10},{10,11},{11... | collective-permute-start | bytes 1105928 | tf_op jit(solution)/shard_map/ppermute | solution.py:18
  37.5 13.0 %collective-permute-start.3 = (bf16[2,4,10,3,768]{4,3,2,1,0:T(4,128)(2,1)}, bf16[2,4,10,3,768]{4,3,2,1,0:T(4,128)(2,1)}, u32[]{:S(2)}, u32[]{:S(2)}) collective-permute-start(bf16[2,4,10,3,768]{4,3,2,1,0:T(4,128)(2,1)} %get-tuple-element.102), channel_id=1, source_target_pairs={{1,0},{2,1},{3,2},{4,3},{5,4},{6,5},{7,6},{9,8},{10,9},{11,10},{12... | collective-permute-start | bytes 1105928 | tf_op jit(solution)/shard_map/ppermute | solution.py:21
  53.6 1.8 %copy-start.3 = (pred[220]{0:T(512)(128)(4,1)S(1)}, pred[220]{0:T(512)(128)(4,1)}, u32[]{:S(2)}) copy-start(pred[220]{0:T(512)(128)(4,1)} %reshape.291) | copy-start | bytes 664
  82.1 1.8 %copy-start.5 = (f32[768]{0:T(1024)S(1)}, f32[768]{0:T(1024)}, u32[]{:S(2)}) copy-start(f32[768]{0:T(1024)} %param.19) | copy-start | bytes 9220
  82.1 1.9 %copy-start.7 = (bf16[768,768]{1,0:T(8,128)(2,1)S(1)}, bf16[768,768]{1,0:T(8,128)(2,1)}, u32[]{:S(2)}) copy-start(bf16[768,768]{1,0:T(8,128)(2,1)} %param.21) | copy-start | bytes 3538948
  84.0 1.5 copy-start.8
  85.3 59.7 %all-gather.3.cloned.1.call-start = ((), (), s32[]{:S(2)}) async-start(), calls=%async_computation | async-start | bytes 1966080 | tf_op jit(solution)/shard_map/all_gather | solution.py:133
  128.4 1.2 copy-start.1
Sparse Core Ops, SparseCore 0:
  85.4 32.0 all-gather.4
  119.3 25.6 all-gather.2
where the time goes:
time: 167 us; the launch traced here: 166 us
  waiting for transfers between devices  63.9 us (38%)
  local copies, waits for them, and re-layouts  35.8 us (21%)
  matrix products  30.5 us (18%)
  between operations  13.7 us (8%)
  starting transfers between devices  11.1 us (7%)
  other arithmetic  10.8 us (6%)
    all_gather x1, waiting for transfers between devices, body(): lax.all_gather(key_time, 'view', axis=0, tiled=True)  28.3 us
    all_gather x1, waiting for transfers between devices, body(): lax.all_gather(value_time, 'view', axis=0, tiled=True)  13.6 us
    dot_general x8, matrix products, project(): result = jnp.dot(flat, weight_matrix, preferred_element_type=jnp.float32)  13.5 us
    ppermute x2, waiting for transfers between devices, padded(): lax.ppermute(lax.slice_in_dim(block, block.shape[dim] - width, None, axis...  13.3 us
    ppermute x2, waiting for transfers between devices, padded(): lax.ppermute(lax.slice_in_dim(block, 0, width, axis=dim), axis, backward)  8.65 us
    ppermute x2, starting transfers between devices, padded(): lax.ppermute(lax.slice_in_dim(block, block.shape[dim] - width, None, axis...  8.27 us
    dynamic_slice x8, local copies, waits for them, and re-layouts, neighbour(): return lax.map(one_view, (queries, keys_wide, values_wide))  8.21 us
    reshape x1, local copies, waits for them, and re-layouts, body(): lax.all_gather(key_time, 'view', axis=0, tiled=True)  5.86 us
  transfers between devices with their start and end apart: 6, of which 6 were waited for; matrix products, arithmetic and copies ran while one was open for 13% of the time, Pallas kernels for 0%

commit v1 on v0

--- a/solution.py
+++ b/solution.py
@@ -130,7 +130,9 @@
         -1, positions, HEADS, HEAD_DIM
     )
     value_heads = (
-        lax.all_gather(value_time, "view", axis=0, tiled=True)
+        jnp.concatenate(
+            lax.all_to_all(jnp.stack([value_time] * lax.axis_size("view")), "view", 0, 0), axis=0
+        )
         .reshape(-1, positions, HEADS, HEAD_DIM)
         .astype(jnp.float32)
     )

time: 167 us -> 160 us (0.958)
  the two profiles are of different devices: /device:TPU:1 before, /device:TPU:102 now
where the time goes in v1:
time: 160 us; the launch traced here: 159 us
  waiting for transfers between devices  49.7 us (31%)
  local copies, waits for them, and re-layouts  36 us (22%)
  matrix products  31.4 us (20%)
  starting transfers between devices  17 us (11%)
  between operations  13.7 us (9%)
  other arithmetic  10.8 us (7%)
    all_to_all x1, waiting for transfers between devices, body(): lax.all_to_all(jnp.stack([value_time] * lax.axis_size('view')), 'view', 0...  24.9 us
    ppermute x2, waiting for transfers between devices, padded(): lax.ppermute(lax.slice_in_dim(block, block.shape[dim] - width, None, axis...  14.3 us
    dot_general x8, matrix products, project(): result = jnp.dot(flat, weight_matrix, preferred_element_type=jnp.float32)  13.6 us
    ppermute x2, waiting for transfers between devices, padded(): lax.ppermute(lax.slice_in_dim(block, 0, width, axis=dim), axis, backward)  10.5 us
    ppermute x2, starting transfers between devices, padded(): lax.ppermute(lax.slice_in_dim(block, block.shape[dim] - width, None, axis...  8.42 us
    dynamic_slice x8, local copies, waits for them, and re-layouts, neighbour(): return lax.map(one_view, (queries, keys_wide, values_wide))  8.21 us
    reshape x1, local copies, waits for them, and re-layouts, body(): lax.all_gather(key_time, 'view', axis=0, tiled=True)  6 us
    dot_general x1, matrix products, body(): new_acc = jnp.einsum('qkph,kphe->qphe', weights, value_heads)  5.5 us
  transfers between devices with their start and end apart: 6, of which 5 were waited for; matrix products, arithmetic and copies ran while one was open for 10% of the time, Pallas kernels for 0%

profile of v1, /device:TPU:102, one launch (start us, length us, event | category | flops | bytes accessed | tf_op | source)
XLA Modules:
  0.0 158.8 jit_solution(7740678959094711113)
XLA Ops:
  6.6 1.3 fusion.40
  7.9 1.9 %fusion.28 = bf16[1,4,4,16,768]{4,3,2,1,0:T(8,128)(2,1)S(1)} fusion(bf16[768,768]{1,0:T(8,128)(2,1)} %param.16, bf16[4,4,16,768]{3,2,1,0:T(8,128)(2,1)} %param.13, f32[768]{0:T(1024)} %param.14, f32[4,4,16]{2,1,0:T(4,128)S(1)} %add_rsqrt_fusion.1), kind=kOutput, calls=%fused_computation.46 | convolution fusion | flops 302972928 | bytes 1970176 | tf_op jit(solution)/shard_map/dot_general | solution.py:34
  9.9 0.5 fusion.29
  10.4 1.1 fusion.45
  11.5 5.0 %collective-permute-start = (bf16[2,4,3,16,768]{4,3,2,1,0:T(8,128)(2,1)}, bf16[2,4,3,16,768]{4,3,2,1,0:T(8,128)(2,1)S(1)}, u32[]{:S(2)}, u32[]{:S(2)}) collective-permute-start(bf16[2,4,3,16,768]{4,3,2,1,0:T(8,128)(2,1)} %get-tuple-element.103), channel_id=1, source_target_pairs={{0,8},{8,16},{16,24},{24,32},{32,40},{40,48},{48,56},{1,9},{9,17},... | collective-permute-start | bytes 1769480 | tf_op jit(solution)/shard_map/ppermute | solution.py:18
  16.5 1.9 %collective-permute-start.1 = (bf16[2,4,3,16,768]{4,3,2,1,0:T(8,128)(2,1)}, bf16[2,4,3,16,768]{4,3,2,1,0:T(8,128)(2,1)S(1)}, u32[]{:S(2)}, u32[]{:S(2)}) collective-permute-start(bf16[2,4,3,16,768]{4,3,2,1,0:T(8,128)(2,1)} %get-tuple-element.104), channel_id=1, source_target_pairs={{8,0},{16,8},{24,16},{32,24},{40,32},{48,40},{56,48},{9,1},{17,9},... | collective-permute-start | bytes 1769480 | tf_op jit(solution)/shard_map/ppermute | solution.py:21
  18.5 0.6 reshape.289
  19.2 10.2 %collective-permute-done = bf16[2,4,3,16,768]{4,3,2,1,0:T(8,128)(2,1)S(1)} collective-permute-done((bf16[2,4,3,16,768]{4,3,2,1,0:T(8,128)(2,1)}, bf16[2,4,3,16,768]{4,3,2,1,0:T(8,128)(2,1)S(1)}, u32[]{:S(2)}, u32[]{:S(2)}) %collective-permute-start) | collective-permute-done | bytes 589856 | tf_op jit(solution)/shard_map/ppermute | solution.py:18
  29.4 5.2 %collective-permute-done.1 = bf16[2,4,3,16,768]{4,3,2,1,0:T(8,128)(2,1)S(1)} collective-permute-done((bf16[2,4,3,16,768]{4,3,2,1,0:T(8,128)(2,1)}, bf16[2,4,3,16,768]{4,3,2,1,0:T(8,128)(2,1)S(1)}, u32[]{:S(2)}, u32[]{:S(2)}) %collective-permute-start.1) | collective-permute-done | bytes 589856 | tf_op jit(solution)/shard_map/ppermute | solution.py:21
  34.6 1.3 pad_maximum_fusion.5
  36.0 3.4 %collective-permute-start.2 = (bf16[2,4,10,3,768]{4,3,2,1,0:T(4,128)(2,1)}, bf16[2,4,10,3,768]{4,3,2,1,0:T(4,128)(2,1)}, u32[]{:S(2)}, u32[]{:S(2)}) collective-permute-start(bf16[2,4,10,3,768]{4,3,2,1,0:T(4,128)(2,1)} %get-tuple-element.101), channel_id=1, source_target_pairs={{0,1},{1,2},{2,3},{3,4},{4,5},{5,6},{6,7},{8,9},{9,10},{10,11},{11... | collective-permute-start | bytes 1105928 | tf_op jit(solution)/shard_map/ppermute | solution.py:18
  39.4 2.4 %collective-permute-start.3 = (bf16[2,4,10,3,768]{4,3,2,1,0:T(4,128)(2,1)}, bf16[2,4,10,3,768]{4,3,2,1,0:T(4,128)(2,1)}, u32[]{:S(2)}, u32[]{:S(2)}) collective-permute-start(bf16[2,4,10,3,768]{4,3,2,1,0:T(4,128)(2,1)} %get-tuple-element.102), channel_id=1, source_target_pairs={{1,0},{2,1},{3,2},{4,3},{5,4},{6,5},{7,6},{9,8},{10,9},{11,10},{12... | collective-permute-start | bytes 1105928 | tf_op jit(solution)/shard_map/ppermute | solution.py:21
  42.0 0.6 broadcast_in_dim.38
  42.6 0.7 sub.85
  43.3 2.6 %convolution_convert_fusion.4 = bf16[4,4,16,768]{3,2,1,0:T(8,128)(2,1)} fusion(bf16[768,768]{1,0:T(8,128)(2,1)} %param.15, bf16[4,4,16,768]{3,2,1,0:T(8,128)(2,1)S(1)} %copy-done.2, f32[768]{0:T(1024)} %param.14, f32[4,4,16]{2,1,0:T(4,128)} %copy-done.6), kind=kOutput, calls=%fused_computation.43 | convolution fusion | flops 302972928 | bytes 1970176 | tf_op jit(solution)/shard_map/dot_general | solution.py:34
  45.9 4.1 %collective-permute-done.2 = bf16[2,4,10,3,768]{4,3,2,1,0:T(4,128)(2,1)} collective-permute-done((bf16[2,4,10,3,768]{4,3,2,1,0:T(4,128)(2,1)}, bf16[2,4,10,3,768]{4,3,2,1,0:T(4,128)(2,1)}, u32[]{:S(2)}, u32[]{:S(2)}) %collective-permute-start.2) | collective-permute-done | bytes 368672 | tf_op jit(solution)/shard_map/ppermute | solution.py:18
  50.0 5.2 %collective-permute-done.3 = bf16[2,4,10,3,768]{4,3,2,1,0:T(4,128)(2,1)} collective-permute-done((bf16[2,4,10,3,768]{4,3,2,1,0:T(4,128)(2,1)}, bf16[2,4,10,3,768]{4,3,2,1,0:T(4,128)(2,1)}, u32[]{:S(2)}, u32[]{:S(2)}) %collective-permute-start.3) | collective-permute-done | bytes 368672 | tf_op jit(solution)/shard_map/ppermute | solution.py:21
  55.2 3.1 %pad_maximum_fusion = bf16[2,4,10,22,768]{4,3,2,1,0:T(8,128)(2,1)S(1)} fusion(bf16[2,4,10,3,768]{4,3,2,1,0:T(4,128)(2,1)} %collective-permute-done.3, bf16[2,4,3,16,768]{4,3,2,1,0:T(8,128)(2,1)S(1)} %collective-permute-done.1, bf16[1,4,4,16,768]{4,3,2,1,0:T(8,128)(2,1)S(1)} %fusion.29, bf16[1,4,4,16,768]{4,3,2,1,0:T(8,128)(2,1)S(1)} %fusion.28, ...), kind=kLoop, calls=%fused_computation.26 | loop fusion | flops 16220160 | bytes 5406720 | tf_op jit(solution)/shard_map/concatenate | solution.py:22
  58.4 1.8 %slice_bitcast_fusion = (bf16[4,10,22,768]{3,2,1,0:T(8,128)(2,1)}, bf16[4,10,22,768]{3,2,1,0:T(8,128)(2,1)}) fusion(bf16[2,4,10,22,768]{4,3,2,1,0:T(8,128)(2,1)S(1)} %pad_maximum_fusion), kind=kLoop, calls=%fused_computation.33 | loop fusion | bytes 5406720 | tf_op jit(solution)/shard_map/squeeze | solution.py:113
  60.2 26.6 %while.11 = (s32[]{:T(128)}, bf16[4,4,16,768]{3,2,1,0:T(8,128)(2,1)}, bf16[4,10,22,768]{3,2,1,0:T(8,128)(2,1)}, bf16[4,4,16,768]{3,2,1,0:T(8,128)(2,1)}, bf16[4,...) while((s32[]{:T(128)}, ...), condition=%wide.region_4.5_spmd.clone, body=%wide.region_1.4_spmd.clone.sunk | while | flops 152731136 | bytes 6633009 | solution.py:86
  60.2 1.1 constant_dynamic-slice_fusion.5
  61.3 0.5 reshape.304
  62.0 0.9 constant_dynamic-slice_fusion.6
  63.1 0.6 fusion.71
  64.0 0.5 reshape.306
  64.6 1.2 fusion.73
  66.2 0.7 constant_dynamic-update-slice_fusion.2
  66.8 1.1 constant_dynamic-slice_fusion.5
  68.0 0.5 reshape.304
  68.6 0.9 constant_dynamic-slice_fusion.6
  69.7 0.6 fusion.71
  70.4 0.3 fusion.72
  70.7 0.5 reshape.306
  71.2 1.2 fusion.73
  72.8 0.7 constant_dynamic-update-slice_fusion.2
  73.5 1.1 constant_dynamic-slice_fusion.5
  74.6 0.5 reshape.304
  75.3 0.9 constant_dynamic-slice_fusion.6
  76.4 0.6 fusion.71
  77.4 0.5 reshape.306
  77.9 1.2 fusion.73
  79.5 0.7 constant_dynamic-update-slice_fusion.2
  80.2 1.1 constant_dynamic-slice_fusion.5
  81.3 0.5 reshape.304
  82.0 0.9 constant_dynamic-slice_fusion.6
  83.0 0.6 fusion.71
  84.0 0.5 reshape.306
  84.6 1.2 fusion.73
  86.2 0.7 constant_dynamic-update-slice_fusion.2
  86.8 1.8 %multiply_reduce_fusion = (f32[4,4,16]{2,1,0:T(4,128)S(1)}, f32[4,4,16,768]{3,2,1,0:T(8,128)S(1)}) fusion(bf16[4,4,16,768]{3,2,1,0:T(8,128)(2,1)} %get-tuple-element.37, bf16[768,768]{1,0:T(8,128)(2,1)S(1)} %copy-done, bf16[4,4,16,768]{3,2,1,0:T(8,128)(2,1)} %param.13), kind=kOutput, calls=%fused_computation.67 | convolution fusion | flops 303169280 | bytes 2753536 | tf_op jit(solution)/shard_map/dot_general | solution.py:34
  88.8 1.2 convolution_convert_fusion.2
  90.2 0.5 convolution_convert_fusion.3
  90.7 1.3 stack.19
  92.0 4.2 %all-to-all-start = ((bf16[4,4,4,16,768]{4,3,2,1,0:T(8,128)(2,1)}), bf16[4,4,4,16,768]{4,3,2,1,0:T(8,128)(2,1)S(1)}, u32[]{:S(2)}, u32[]{:S(2)}) async-start(bf16[4,4,4,16,768]{4,3,2,1,0:T(8,128)(2,1)} %stack.19), calls=%async_computation | async-start | bytes 3145728 | tf_op jit(solution)/shard_map/all_to_all | solution.py:134
  96.2 2.6 %convolution_convert_fusion.1 = bf16[4,4,16,768]{3,2,1,0:T(8,128)(2,1)} fusion(bf16[4,4,16,768]{3,2,1,0:T(8,128)(2,1)} %copy-done.4, bf16[768,768]{1,0:T(8,128)(2,1)} %param.20), kind=kOutput, calls=%fused_computation.40 | convolution fusion | flops 302186496 | bytes 1966080 | tf_op jit(solution)/shard_map/dot_general | solution.py:34
  98.8 2.4 %reshape.288 = bf16[4,64,12,64]{3,2,1,0:T(8,128)(2,1)} reshape(bf16[4,4,16,768]{3,2,1,0:T(8,128)(2,1)} %convolution_convert_fusion.1) | data formatting | bytes 786432 | tf_op jit(solution)/shard_map/reshape | solution.py:127
  101.2 24.9 %all-to-all-done = bf16[4,4,4,16,768]{4,3,2,1,0:T(8,128)(2,1)S(1)} async-done(((bf16[4,4,4,16,768]{4,3,2,1,0:T(8,128)(2,1)}), bf16[4,4,4,16,768]{4,3,2,1,0:T(8,128)(2,1)S(1)}, u32[]{:S(2)}, u32[]{:S(2)}) %all-to-all-start) | async-done | bytes 1572896 | tf_op jit(solution)/shard_map/all_to_all | solution.py:134
  126.2 3.8 %reshape_reshape.3 = bf16[16,64,12,64]{3,2,1,0:T(8,128)(2,1)} reshape(bf16[4,4,4,16,768]{4,3,2,1,0:T(8,128)(2,1)S(1)} %all-to-all-done) | data formatting | bytes 3145728 | tf_op jit(solution)/shard_map/reshape;reshape | solution.py:136
  130.0 6.0 %reshape.287 = bf16[16,64,12,64]{3,2,1,0:T(8,128)(2,1)} reshape(bf16[16,4,16,768]{3,2,1,0:T(8,128)(2,1)} %all-gather.2.cloned.1.call-done) | data formatting | bytes 3145728 | tf_op jit(solution)/shard_map/reshape | solution.py:129
  136.0 5.1 %bitcast_reduce_fusion = (f32[4,64,12]{0,2,1:T(8,128)S(1)}, f32[64,12,16,4]{2,3,1,0:T(4,128)S(1)}) fusion(bf16[4,64,12,64]{3,2,1,0:T(8,128)(2,1)S(1)} %copy-done.3, bf16[16,64,12,64]{3,2,1,0:T(8,128)(2,1)} %reshape.287), kind=kOutput, calls=%fused_computation.29 | convolution fusion | flops 6386688 | bytes 2174976 | tf_op jit(solution)/shard_map/qphe,kphe->qkph/dot_general | solution.py:140
  141.2 1.9 %fusion.30 = f32[4,64,12]{0,2,1:T(8,128)S(1)} fusion(f32[64,12,16,4]{2,3,1,0:T(4,128)S(1)} %get-tuple-element.108, f32[4,64,12]{0,2,1:T(8,128)S(1)} %broadcast_maximum_fusion), kind=kLoop, calls=%fused_computation.48 | loop fusion | flops 95232 | bytes 221184 | tf_op jit(solution)/shard_map/reduce_sum | solution.py:145
  143.1 5.5 %fusion.19 = bf16[4,64,12,64]{3,0,2,1:T(4,128)(2,1)S(1)} fusion(bf16[16,64,12,64]{3,2,1,0:T(8,128)(2,1)S(1)} %copy-done.1, f32[64,12,16,4]{2,3,1,0:T(4,128)S(1)} %get-tuple-element.108, f32[4,64,12]{0,2,1:T(8,128)S(1)} %fusion.30, f32[4,64,12]{0,2,1:T(8,128)S(1)} %broadcast_maximum_fusion), kind=kOutput, calls=%fused_computation.31 | convolution fusion | flops 6733824 | bytes 2187264 | tf_op jit(solution)/shard_map/qkph,kphe->qphe/dot_general | solution.py:146
  148.8 0.6 convert_element_type.76
  149.5 2.5 %fusion.27 = bf16[4,4,16,768]{3,2,1,0:T(8,128)(2,1)} fusion(f32[4,4,16,768]{3,2,1,0:T(8,128)S(1)} %get-tuple-element.106, bf16[4,4,16,768]{3,2,1,0:T(8,128)(2,1)S(1)} %convert_element_type.76, bf16[768,768]{1,0:T(8,128)(2,1)} %param.23), kind=kOutput, calls=%fused_computation.39 | convolution fusion | flops 302383104 | bytes 2752512 | tf_op jit(solution)/shard_map/dot_general | solution.py:34
  (59 shorter events, 4.7 us)
Async XLA Ops:
  6.5 80.3 %copy-start = (bf16[768,768]{1,0:T(8,128)(2,1)S(1)}, bf16[768,768]{1,0:T(8,128)(2,1)}, u32[]{:S(2)}) copy-start(bf16[768,768]{1,0:T(8,128)(2,1)} %param.18) | copy-start | bytes 3538948
  6.5 3.3 %copy-start.2 = (bf16[4,4,16,768]{3,2,1,0:T(8,128)(2,1)S(1)}, bf16[4,4,16,768]{3,2,1,0:T(8,128)(2,1)}, u32[]{:S(2)}) copy-start(bf16[4,4,16,768]{3,2,1,0:T(8,128)(2,1)} %param.13) | copy-start | bytes 1179652
  6.5 3.3 %copy-start.11 = (f32[768]{0:T(1024)S(1)}, f32[768]{0:T(1024)}, u32[]{:S(2)}) copy-start(f32[768]{0:T(1024)} %param.14) | copy-start | bytes 9220
  6.5 123.5 %all-gather.2.cloned.1.call-start = ((), (), s32[]{:S(2)}) async-start(), calls=%async_computation.1 | async-start | bytes 1966080 | tf_op jit(solution)/shard_map/all_gather | solution.py:129
  6.5 3.3 %copy-start.8 = (bf16[768,768]{1,0:T(8,128)(2,1)S(1)}, bf16[768,768]{1,0:T(8,128)(2,1)}, u32[]{:S(2)}) copy-start(bf16[768,768]{1,0:T(8,128)(2,1)} %param.17) | copy-start | bytes 3538948
  7.9 2.5 %copy-start.6 = (f32[4,4,16]{2,1,0:T(4,128)}, f32[4,4,16]{2,1,0:T(4,128)S(1)}, u32[]{:S(2)}) copy-start(f32[4,4,16]{2,1,0:T(4,128)S(1)} %add_rsqrt_fusion.1) | copy-start | bytes 3076
  11.5 17.9 %collective-permute-start = (bf16[2,4,3,16,768]{4,3,2,1,0:T(8,128)(2,1)}, bf16[2,4,3,16,768]{4,3,2,1,0:T(8,128)(2,1)S(1)}, u32[]{:S(2)}, u32[]{:S(2)}) collective-permute-start(bf16[2,4,3,16,768]{4,3,2,1,0:T(8,128)(2,1)} %get-tuple-element.103), channel_id=1, source_target_pairs={{0,8},{8,16},{16,24},{24,32},{32,40},{40,48},{48,56},{1,9},{9,17},... | collective-permute-start | bytes 1769480 | tf_op jit(solution)/shard_map/ppermute | solution.py:18
  16.5 18.1 %collective-permute-start.1 = (bf16[2,4,3,16,768]{4,3,2,1,0:T(8,128)(2,1)}, bf16[2,4,3,16,768]{4,3,2,1,0:T(8,128)(2,1)S(1)}, u32[]{:S(2)}, u32[]{:S(2)}) collective-permute-start(bf16[2,4,3,16,768]{4,3,2,1,0:T(8,128)(2,1)} %get-tuple-element.104), channel_id=1, source_target_pairs={{8,0},{16,8},{24,16},{32,24},{40,32},{48,40},{56,48},{9,1},{17,9},... | collective-permute-start | bytes 1769480 | tf_op jit(solution)/shard_map/ppermute | solution.py:21
  36.0 14.0 %collective-permute-start.2 = (bf16[2,4,10,3,768]{4,3,2,1,0:T(4,128)(2,1)}, bf16[2,4,10,3,768]{4,3,2,1,0:T(4,128)(2,1)}, u32[]{:S(2)}, u32[]{:S(2)}) collective-permute-start(bf16[2,4,10,3,768]{4,3,2,1,0:T(4,128)(2,1)} %get-tuple-element.101), channel_id=1, source_target_pairs={{0,1},{1,2},{2,3},{3,4},{4,5},{5,6},{6,7},{8,9},{9,10},{10,11},{11... | collective-permute-start | bytes 1105928 | tf_op jit(solution)/shard_map/ppermute | solution.py:18
  39.4 15.9 %collective-permute-start.3 = (bf16[2,4,10,3,768]{4,3,2,1,0:T(4,128)(2,1)}, bf16[2,4,10,3,768]{4,3,2,1,0:T(4,128)(2,1)}, u32[]{:S(2)}, u32[]{:S(2)}) collective-permute-start(bf16[2,4,10,3,768]{4,3,2,1,0:T(4,128)(2,1)} %get-tuple-element.102), channel_id=1, source_target_pairs={{1,0},{2,1},{3,2},{4,3},{5,4},{6,5},{7,6},{9,8},{10,9},{11,10},{12... | collective-permute-start | bytes 1105928 | tf_op jit(solution)/shard_map/ppermute | solution.py:21
  58.4 1.8 %copy-start.5 = (pred[220]{0:T(512)(128)(4,1)S(1)}, pred[220]{0:T(512)(128)(4,1)}, u32[]{:S(2)}) copy-start(pred[220]{0:T(512)(128)(4,1)} %reshape.289) | copy-start | bytes 664
  86.8 1.8 %copy-start.7 = (f32[768]{0:T(1024)S(1)}, f32[768]{0:T(1024)}, u32[]{:S(2)}) copy-start(f32[768]{0:T(1024)} %param.19) | copy-start | bytes 9220
  86.8 1.9 %copy-start.9 = (bf16[768,768]{1,0:T(8,128)(2,1)S(1)}, bf16[768,768]{1,0:T(8,128)(2,1)}, u32[]{:S(2)}) copy-start(bf16[768,768]{1,0:T(8,128)(2,1)} %param.21) | copy-start | bytes 3538948
  88.8 1.9 %copy-start.4 = (bf16[4,4,16,768]{3,2,1,0:T(8,128)(2,1)}, bf16[4,4,16,768]{3,2,1,0:T(8,128)(2,1)S(1)}, u32[]{:S(2)}) copy-start(bf16[4,4,16,768]{3,2,1,0:T(8,128)(2,1)S(1)} %multiply_convert_fusion) | copy-start | bytes 1179652
  88.8 1.4 copy-start.10
  92.0 34.2 %all-to-all-start = ((bf16[4,4,4,16,768]{4,3,2,1,0:T(8,128)(2,1)}), bf16[4,4,4,16,768]{4,3,2,1,0:T(8,128)(2,1)S(1)}, u32[]{:S(2)}, u32[]{:S(2)}) async-start(bf16[4,4,4,16,768]{4,3,2,1,0:T(8,128)(2,1)} %stack.19), calls=%async_computation | async-start | bytes 3145728 | tf_op jit(solution)/shard_map/all_to_all | solution.py:134
  130.0 6.0 %copy-start.3 = (bf16[4,64,12,64]{3,2,1,0:T(8,128)(2,1)S(1)}, bf16[4,64,12,64]{3,2,1,0:T(8,128)(2,1)}, u32[]{:S(2)}) copy-start(bf16[4,64,12,64]{3,2,1,0:T(8,128)(2,1)} %reshape.288) | copy-start | bytes 1179652
  136.0 7.1 %copy-start.1 = (bf16[16,64,12,64]{3,2,1,0:T(8,128)(2,1)S(1)}, bf16[16,64,12,64]{3,2,1,0:T(8,128)(2,1)}, u32[]{:S(2)}) copy-start(bf16[16,64,12,64]{3,2,1,0:T(8,128)(2,1)} %reshape_reshape.3) | copy-start | bytes 4718596
Sparse Core Ops, SparseCore 0:
  90.2 33.4 all-gather.1
